TPU v7x, 32 devices: a whole 2x2x4 slice. The times are simulated.
32 devices in a mesh: chan: 8 (over y, x, core), tm: 4 (over z).
Axes of the slice: x: 2, y: 2, z: 4, core: 2. Of those that a mesh axis runs over, the one named last changes fastest.
Arguments:
- records: float32 [2560, 4, 7936], P('chan', 'tm'), may hold values from -6 to 6
- offsets: int32 [4], P('tm'), may hold values from 0 to 256
Outputs:
- correlations: float32 [2, 640, 2, 20480], P(None, 'tm', None, 'chan')
All inputs are finite; a program needn't handle non-finite values.
Results may differ from a plain program's by a relative error of at most 0.0001.
Values sent between devices are 32-bit elements; how exact they have to be, the bound alone decides.
A program may use at most 128 MiB of HBM per device.

v0:
```python
import functools
import math

import jax
import jax.numpy as jnp
import numpy as np
from jax import lax
from jax.experimental import pallas as pl
from jax.experimental.pallas import tpu as pltpu
from jax.sharding import PartitionSpec as P

MESH = pl.DeviceIdType.MESH
SRC = 8
LEN = 7680
FB = 640
FLO = 64
SMOOTH = 64
ROUNDS = 2
M = 15
L = LEN // M
Q0 = FLO // M
NQ = 48
BASE = 16
START = BASE + M * Q0 - FLO
ROWS = START + M // 2 + M * (NQ - 1) + 5
LANES = 128
PARTS = LEN // LANES
CT = 64
WIDE = CT * SRC
KB = 40


def split(x):
    hi = x.astype(jnp.bfloat16)
    return hi, (x - hi.astype(jnp.float32)).astype(jnp.bfloat16)


def twice(x):
    return jnp.concatenate(split(x), 1)


def tables(n):
    a = np.arange(L)
    q = Q0 + np.arange(NQ)
    angle = 2.0 * math.pi * ((q[:, None] * a[None, :]) % L) / L
    full = np.concatenate([np.cos(angle), np.sin(angle)]).astype(np.float32)
    hi = full.astype(jnp.bfloat16)
    lo = (full - hi.astype(np.float32)).astype(jnp.bfloat16)
    both = np.concatenate([hi, lo])
    r = np.arange(1, M // 2 + 1)
    turn = 2.0 * math.pi * (r[:, None] * a[None, :]) / LEN
    twiddle = np.stack([np.cos(turn), np.sin(turn)], 1).reshape(2 * len(r), L)
    twiddle = np.repeat(twiddle[:, None, :], 8, 1).astype(np.float32)
    k = np.arange(FB)
    band = (np.abs(k[:, None] - k[None, :]) <= SMOOTH).astype(jnp.bfloat16)
    lane = np.arange(LANES)[:, None]
    col = np.arange(2 * WIDE)[None, :]
    spread = lane == (col // WIDE) * CT + (col % WIDE) // SRC
    spread = np.concatenate([spread, spread]).astype(jnp.bfloat16)
    packed = np.arange(pack_width(n))[:, None]
    col = np.arange(2 * n * LANES)[None, :]
    fan = packed == (col // LANES) * SRC + col % SRC
    fan = np.concatenate([fan, fan]).astype(jnp.bfloat16)
    return twiddle, both, band, spread, fan


def pack_width(n):
    return -(-2 * SRC * n // LANES) * LANES


C3 = math.sqrt(3.0) / 2.0
C51, C52 = math.cos(2 * math.pi / 5), math.cos(4 * math.pi / 5)
S51, S52 = math.sin(2 * math.pi / 5), math.sin(4 * math.pi / 5)


def dft3(x0, x1, x2):
    t = x1 + x2
    return x0 + t, x0 - 0.5 * t, C3 * (x2 - x1)


def dft5(x):
    t1, t2 = x[1] + x[4], x[2] + x[3]
    d1, d2 = x[1] - x[4], x[2] - x[3]
    re0 = x[0] + t1 + t2
    re1 = x[0] + C51 * t1 + C52 * t2
    re2 = x[0] + C52 * t1 + C51 * t2
    im1 = -(S51 * d1 + S52 * d2)
    im2 = S51 * d2 - S52 * d1
    return re0, re1, im1, re2, im2


def dft15(x):
    columns = [dft3(*[x[(5 * n1 + 3 * n2) % 15] for n1 in range(3)]) for n2 in range(5)]
    z = dft5([c[0] for c in columns])
    u = dft5([c[1] for c in columns])
    v = dft5([c[2] for c in columns])
    out = {}
    out[(0, 0)] = (z[0], None)
    out[(0, 1)] = (z[1], z[2])
    out[(0, 2)] = (z[3], z[4])
    out[(1, 0)] = (u[0], v[0])
    for j, (b, s) in ((1, (1, 2)), (2, (3, 4))):
        out[(1, j)] = (u[b] - v[s], u[s] + v[b])
        out[(1, 5 - j)] = (u[b] + v[s], v[b] - u[s])
    bins = [None] * 8
    for (k1, k2), (re, im) in out.items():
        k = (10 * k1 + 6 * k2) % 15
        if k <= 7:
            bins[k] = (re, im)
        else:
            bins[15 - k] = (re, -im)
    return bins


def first_stage(rows, base, off, x_ref, twiddle_ref, hi_ref, lo_ref):
    lane = lax.broadcasted_iota(jnp.int32, (16, LANES), 1)
    extra = rows - PARTS

    def put(row, c0, a0, value):
        hi, lo = split(value)
        hi_ref[pl.ds(row * CT + c0, 16), pl.ds(a0, LANES)] = hi
        lo_ref[pl.ds(row * CT + c0, 16), pl.ds(a0, LANES)] = lo

    def block(i, carry):
        c0 = pl.multiple_of(i * 16, 16)

        def load(j):
            return x_ref[pl.ds(base + c0 * rows + j, 16, stride=rows), :]

        for t in range(L // LANES):
            x = []
            for b in range(M):
                j = b * (L // LANES) + t
                value = load(j)
                if j < extra:
                    value = jnp.where(lane + j * LANES < off, load(j + PARTS), value)
                x.append(value)
            bins = dft15(x)
            a0 = t * LANES
            put(14, c0, a0, bins[0][0])
            for r in range(1, 8):
                re, im = bins[r]
                cos = twiddle_ref[2 * r - 2, :, a0 : a0 + LANES]
                sin = twiddle_ref[2 * r - 1, :, a0 : a0 + LANES]
                cos = jnp.concatenate([cos, cos], 0)
                sin = jnp.concatenate([sin, sin], 0)
                put(2 * r - 2, c0, a0, re * cos + im * sin)
                put(2 * r - 1, c0, a0, im * cos - re * sin)
        return carry

    lax.fori_loop(0, CT // 16, block, 0)


def second_stage(both_ref, hi_ref, lo_ref, w_ref):
    nt = (((1,), (1,)), ((), ()))
    low = lax.broadcasted_iota(jnp.int32, (NQ, LANES), 1) < CT

    def second(row, count):
        window = slice(row * CT, (row + count) * CT)
        p = lax.dot_general(both_ref[...], hi_ref[window, :], nt, preferred_element_type=jnp.float32)
        s = lax.dot_general(both_ref[: 2 * NQ, :], lo_ref[window, :], nt, preferred_element_type=jnp.float32)
        z = p[: 2 * NQ] + p[2 * NQ :] + s
        return z[:NQ], z[NQ:]

    for pair in range(4):
        zc, zs = second(4 * pair, min(4, M - 4 * pair))
        for i in range(2):
            r = 2 * pair + 1 + i
            if r == 8:
                w_ref[pl.ds(START, NQ, stride=M), :] = jnp.concatenate([zc[:, LANES:], -zs[:, LANES:]], 1)
                continue
            c = zc[:, i * LANES : (i + 1) * LANES]
            s = pltpu.roll(zs[:, i * LANES : (i + 1) * LANES], CT, 1)
            w_ref[pl.ds(START + r, NQ, stride=M), :] = c + jnp.where(low, s, -s)
            w_ref[pl.ds(START - r, NQ, stride=M), :] = jnp.where(low, c, -c) - s


def normalised(band_ref, w_ref):
    spec = w_ref[BASE : BASE + FB, :]
    power = spec * spec
    amp = jnp.sqrt(power + pltpu.roll(power, CT, 1))
    high = amp.astype(jnp.bfloat16).astype(jnp.float32)
    low = lax.broadcasted_iota(jnp.int32, (FB, LANES), 1) < CT
    parts = jnp.where(low, high, amp - high).astype(jnp.bfloat16)
    total = jnp.dot(band_ref[...], parts, preferred_element_type=jnp.float32)
    total = total + pltpu.roll(total, CT, 1)
    k = lax.broadcasted_iota(jnp.int32, (FB, LANES), 0)
    count = jnp.minimum(k + SMOOTH, FB - 1) - jnp.maximum(k - SMOOTH, 0) + 1
    count = count.astype(jnp.float32)
    return spec * (count / (total + 1e-06 * count))


def kernel(n, nc, rows, nt, off_ref, x_hbm, tw_hbm, both_hbm, band_hbm, spread_hbm, fan_hbm, o_hbm,
           x_ref, tw_ref, both_ref, band_ref, spread_ref, fan_ref, hi_ref, lo_ref, w_ref, white, recv,
           src_send, src_recv, b_ref, a_ref, stage,
           x_sem, const_sem, send_sem, recv_sem, ssend_sem, srecv_sem, out_sem):
    me = lax.axis_index("tm")
    blk = lax.axis_index("chan")
    bins = FB // n
    nsub = bins // KB
    off = off_ref[0]

    def fetch(t):
        part = pl.ds(t * CT * rows, CT * rows)
        return pltpu.make_async_copy(x_hbm.at[part, :], x_ref.at[part, :], x_sem.at[t])

    pairs = ((tw_hbm, tw_ref), (both_hbm, both_ref), (band_hbm, band_ref), (spread_hbm, spread_ref), (fan_hbm, fan_ref))
    consts = [pltpu.make_async_copy(src, dst, const_sem.at[i]) for i, (src, dst) in enumerate(pairs)]
    fetch(0).start()
    for c in consts[:3]:
        c.start()
    for t in range(1, nt):
        fetch(t).start()
    for c in consts[3:]:
        c.start()

    barrier = pltpu.get_barrier_semaphore()
    chan_steps = sorted({s % nc for r in range(1, ROUNDS + 1) for s in (r, -r)} - {0})
    for sh in range(1, n):
        pl.semaphore_signal(barrier, inc=1, device_id={"tm": lax.rem(me + sh, n)}, device_id_type=MESH)
    for s in chan_steps:
        pl.semaphore_signal(barrier, inc=1, device_id={"chan": lax.rem(blk + s, nc)}, device_id_type=MESH)

    def exchange(t, j, sh):
        peer = lax.rem(me + sh, n)
        return pltpu.make_async_remote_copy(
            src_ref=white.at[t, pl.ds(pl.multiple_of(peer * bins + j * KB, 8), KB), :],
            dst_ref=recv.at[sh - 1, t, pl.ds(pl.multiple_of(j * KB, 8), KB), :],
            send_sem=send_sem.at[t, sh - 1, j],
            recv_sem=recv_sem.at[t, sh - 1, j],
            device_id={"tm": peer},
            device_id_type=MESH,
        )

    order = list(range(2, n)) + [1]

    def transform(t, carry):
        fetch(t).wait()

        @pl.when(t == 0)
        def _():
            consts[0].wait()

        first_stage(rows, t * CT * rows, off, x_ref, tw_ref, hi_ref, lo_ref)

        @pl.when(t == 0)
        def _():
            consts[1].wait()

        second_stage(both_ref, hi_ref, lo_ref, w_ref)

        @pl.when(t == 0)
        def _():
            consts[2].wait()

        white[t] = normalised(band_ref, w_ref)

        @pl.when(t == 0)
        def _():
            pl.semaphore_wait(barrier, n - 1 + len(chan_steps))

        for j in range(nsub):
            for sh in order:
                exchange(t, j, sh).start()
        return carry

    lax.fori_loop(0, nt, transform, 0)

    mine = pl.multiple_of(me * bins, 8)
    for j in range(nsub):
        for sh in order:
            exchange(0, j, sh).wait_recv()
    lane = lax.broadcasted_iota(jnp.int32, (bins, LANES), 1)
    for tile in range(src_send.shape[1] // LANES):
        packed = jnp.zeros((bins, LANES), jnp.float32)
        for sh in range(n):
            at = sh * 2 * SRC - tile * LANES
            if not 0 <= at < LANES:
                continue
            value = white[0, pl.ds(mine, bins), :] if sh == 0 else recv[sh - 1, 0]
            re = pltpu.roll(value, at, 1) if at else value
            im = pltpu.roll(value, (at + SRC - CT) % LANES, 1)
            packed = jnp.where((lane >= at) & (lane < at + SRC), re, packed)
            packed = jnp.where((lane >= at + SRC) & (lane < at + 2 * SRC), im, packed)
        src_send[:, tile * LANES : (tile + 1) * LANES] = packed

    def source(r):
        return pltpu.make_async_remote_copy(
            src_ref=src_send,
            dst_ref=src_recv.at[r - 1],
            send_sem=ssend_sem.at[r - 1],
            recv_sem=srecv_sem.at[r - 1],
            device_id={"chan": lax.rem(blk + nc - r, nc)},
            device_id_type=MESH,
        )

    for r in range(1, ROUNDS + 1):
        source(r).start()
    for c in consts[3:]:
        c.wait()
    for r in range(1, ROUNDS + 1):
        source(r).wait_recv()
        b_ref[r - 1] = jnp.dot(twice(src_recv[r - 1]), fan_ref[...], preferred_element_type=jnp.float32) * (1.0 / n)

    def place(t, j, slot):
        return pltpu.make_async_copy(
            stage.at[slot],
            o_hbm.at[:, pl.ds(pl.multiple_of(j * KB, 8), KB), :, pl.ds(pl.multiple_of(t * WIDE, LANES), WIDE)],
            out_sem.at[slot],
        )

    def pairing(u, carry):
        t = lax.div(u, nsub)
        j = lax.rem(u, nsub)
        slot = lax.rem(u, 2)

        @pl.when(t > 0)
        def _():
            for sh in order:
                exchange(t, j, sh).wait_recv()

        k0 = pl.multiple_of(j * KB, 8)
        a = [white[t, pl.ds(pl.multiple_of(mine + k0, 8), KB), :]]
        a += [recv[sh - 1, t, pl.ds(k0, KB), :] for sh in range(1, n)]
        a_ref[...] = jnp.dot(twice(jnp.concatenate(a, 0)), spread_ref[...], preferred_element_type=jnp.float32)

        @pl.when(u >= 2)
        def _():
            place(t, j, slot).wait()

        def group(g, carry):
            g8 = pl.multiple_of(g * 8, 8)
            b = [[[b_ref[rnd, pl.ds(pl.multiple_of(k0 + g8, 8), 8), (2 * w + p) * LANES : (2 * w + p + 1) * LANES]
                   for p in range(2)] for w in range(n)] for rnd in range(ROUNDS)]
            for tile in range(WIDE // LANES):
                lanes = slice(tile * LANES, (tile + 1) * LANES)
                far = slice(WIDE + tile * LANES, WIDE + (tile + 1) * LANES)
                ar = [a_ref[pl.ds(w * KB + g8, 8), lanes] for w in range(n)]
                ai = [a_ref[pl.ds(w * KB + g8, 8), far] for w in range(n)]
                for rnd in range(ROUNDS):
                    real = imag = None
                    for w in range(n):
                        br, bi = b[rnd][w]
                        p = ar[w] * br + ai[w] * bi
                        q = ai[w] * br - ar[w] * bi
                        real = p if real is None else real + p
                        imag = q if imag is None else imag + q
                    stage[slot, rnd, pl.ds(g8, 8), 0, lanes] = real
                    stage[slot, rnd, pl.ds(g8, 8), 1, lanes] = imag
            return carry

        lax.fori_loop(0, KB // 8, group, 0)
        place(t, j, slot).start()
        return carry

    lax.fori_loop(0, nt * nsub, pairing, 0)

    for r in range(1, ROUNDS + 1):
        source(r).wait_send()

    def drain(t, carry):
        for j in range(nsub):
            for sh in order:
                exchange(t, j, sh).wait_send()
        return carry

    lax.fori_loop(0, nt, drain, 0)
    for u in range(nt * nsub - 2, nt * nsub):
        place(u // nsub, u % nsub, u % 2).wait()


def shards(records, offsets):
    chans = records.shape[0]
    n, nc = lax.axis_size("tm"), lax.axis_size("chan")
    rows = records.shape[2] // LANES
    nt = chans // CT
    bins = FB // n
    nsub = bins // KB
    assert records.shape[1] == 1 and chans % CT == 0 and bins % KB == 0
    flat = records.reshape(chans * rows, LANES)
    consts = [jnp.asarray(c) for c in tables(n)]
    anyspace = pl.BlockSpec(memory_space=pl.ANY)
    f32, bf16 = jnp.float32, jnp.bfloat16
    return pl.pallas_call(
        functools.partial(kernel, n, nc, rows, nt),
        in_specs=[pl.BlockSpec(memory_space=pltpu.SMEM)] + [anyspace] * 6,
        out_specs=anyspace,
        out_shape=jax.ShapeDtypeStruct((ROUNDS, bins, 2, chans * SRC), f32),
        scratch_shapes=[
            pltpu.VMEM((chans * rows, LANES), f32),
            *[pltpu.VMEM(c.shape, c.dtype) for c in consts],
            pltpu.VMEM((M * CT, L), bf16),
            pltpu.VMEM((M * CT, L), bf16),
            pltpu.VMEM((ROWS + 8, LANES), f32),
            pltpu.VMEM((nt, FB, LANES), f32),
            pltpu.VMEM((n - 1, nt, bins, LANES), f32),
            pltpu.VMEM((bins, pack_width(n)), f32),
            pltpu.VMEM((ROUNDS, bins, pack_width(n)), f32),
            pltpu.VMEM((ROUNDS, bins, 2 * n * LANES), f32),
            pltpu.VMEM((n * KB, 2 * WIDE), f32),
            pltpu.VMEM((2, ROUNDS, KB, 2, WIDE), f32),
            pltpu.SemaphoreType.DMA((nt,)),
            pltpu.SemaphoreType.DMA((5,)),
            pltpu.SemaphoreType.DMA((nt, n - 1, nsub)),
            pltpu.SemaphoreType.DMA((nt, n - 1, nsub)),
            pltpu.SemaphoreType.DMA((ROUNDS,)),
            pltpu.SemaphoreType.DMA((ROUNDS,)),
            pltpu.SemaphoreType.DMA((2,)),
        ],
        compiler_params=pltpu.CompilerParams(
            collective_id=0, has_side_effects=True, vmem_limit_bytes=60 << 20
        ),
        name="correlate",
    )(offsets, flat, *consts)


def solution(mesh):
    return jax.shard_map(
        shards,
        mesh=mesh,
        in_specs=(P("chan", "tm", None), P("tm")),
        out_specs=P(None, "tm", None, "chan"),
        check_vma=False,
    )
```

profile of v0, /device:TPU:0, one launch (start us, length us, event | category | flops | bytes accessed | tf_op | source)
XLA Modules:
  0.0 55.0 jit_solution(11677945516571842098)
XLA Ops:
  0.7 46.5 %correlate.1 = f32[2,160,2,2560]{3,2,1,0:T(2,128)} custom-call(s32[1]{0:T(128)S(6)} %copy.9.off_ref, f32[19840,128]{1,0:T(8,128)} %bitcast.1, f32[14,8,512]{2,1,0:T(8,128)} %constant.10.clone.tw_hbm, bf16[192,512]{1,0:T(8,128)(2,1)} %constant.11.clone.both_hbm, bf16[640,640]{1,0:T(8,128)(2,1)} %constant.12.clone.band_hbm, ...), custom_call_target="tpu_custom_call" | custom-call | tf_op jit(solution)/shard_map/correlate/pallas_call | solution.py:384
  47.1 7.9 %copy.10 = f32[2,160,2,2560]{3,2,1,0:T(2,128)} copy(f32[2,160,2,2560]{3,2,1,0:T(2,128)} %correlate.1) | data formatting | bytes 13107200
where the time goes:
time: 55.2 us; the launch traced here: 55 us
  Pallas kernels  46.5 us (84%)
  local copies, waits for them, and re-layouts  7.9 us (14%)
  between operations  0.66 us (1%)
    pallas_call x1, Pallas kernels, shards(): pl.pallas_call(functools.partial(kernel, n, nc, rows, nt), in_specs=[pl.B...  46.5 us
    unnamed x1, local copies, waits for them, and re-layouts  7.9 us

commit v1 on v0

--- a/solution.py
+++ b/solution.py
@@ -190,10 +190,10 @@
     return spec * (count / (total + 1e-06 * count))
 
 
-def kernel(n, nc, rows, nt, off_ref, x_hbm, tw_hbm, both_hbm, band_hbm, spread_hbm, fan_hbm, o_hbm,
+def kernel(n, nc, rows, nt, off_ref, x_hbm, tw_hbm, both_hbm, band_hbm, spread_hbm, fan_hbm, o_ref,
            x_ref, tw_ref, both_ref, band_ref, spread_ref, fan_ref, hi_ref, lo_ref, w_ref, white, recv,
-           src_send, src_recv, b_ref, a_ref, stage,
-           x_sem, const_sem, send_sem, recv_sem, ssend_sem, srecv_sem, out_sem):
+           src_send, src_recv, b_ref, a_ref,
+           x_sem, const_sem, send_sem, recv_sem, ssend_sem, srecv_sem):
     me = lax.axis_index("tm")
     blk = lax.axis_index("chan")
     bins = FB // n
@@ -302,17 +302,9 @@
         source(r).wait_recv()
         b_ref[r - 1] = jnp.dot(twice(src_recv[r - 1]), fan_ref[...], preferred_element_type=jnp.float32) * (1.0 / n)
 
-    def place(t, j, slot):
-        return pltpu.make_async_copy(
-            stage.at[slot],
-            o_hbm.at[:, pl.ds(pl.multiple_of(j * KB, 8), KB), :, pl.ds(pl.multiple_of(t * WIDE, LANES), WIDE)],
-            out_sem.at[slot],
-        )
-
     def pairing(u, carry):
         t = lax.div(u, nsub)
         j = lax.rem(u, nsub)
-        slot = lax.rem(u, 2)
 
         @pl.when(t > 0)
         def _():
@@ -323,10 +315,6 @@
         a = [white[t, pl.ds(pl.multiple_of(mine + k0, 8), KB), :]]
         a += [recv[sh - 1, t, pl.ds(k0, KB), :] for sh in range(1, n)]
         a_ref[...] = jnp.dot(twice(jnp.concatenate(a, 0)), spread_ref[...], preferred_element_type=jnp.float32)
-
-        @pl.when(u >= 2)
-        def _():
-            place(t, j, slot).wait()
 
         def group(g, carry):
             g8 = pl.multiple_of(g * 8, 8)
@@ -345,12 +333,11 @@
                         q = ai[w] * br - ar[w] * bi
                         real = p if real is None else real + p
                         imag = q if imag is None else imag + q
-                    stage[slot, rnd, pl.ds(g8, 8), 0, lanes] = real
-                    stage[slot, rnd, pl.ds(g8, 8), 1, lanes] = imag
+                    o_ref[t, rnd, pl.ds(pl.multiple_of(k0 + g8, 8), 8), 0, lanes] = real
+                    o_ref[t, rnd, pl.ds(pl.multiple_of(k0 + g8, 8), 8), 1, lanes] = imag
             return carry
 
         lax.fori_loop(0, KB // 8, group, 0)
-        place(t, j, slot).start()
         return carry
 
     lax.fori_loop(0, nt * nsub, pairing, 0)
@@ -365,8 +352,18 @@
         return carry
 
     lax.fori_loop(0, nt, drain, 0)
-    for u in range(nt * nsub - 2, nt * nsub):
-        place(u // nsub, u % nsub, u % 2).wait()
+
+
+def write_out(nt, x_ref, o_hbm, sem):
+    copies = [
+        pltpu.make_async_copy(x_ref.at[t, rnd], o_hbm.at[rnd, :, :, pl.ds(t * WIDE, WIDE)], sem.at[t, rnd])
+        for t in range(nt)
+        for rnd in range(ROUNDS)
+    ]
+    for c in copies:
+        c.start()
+    for c in copies:
+        c.wait()
 
 
 def shards(records, offsets):
@@ -381,11 +378,12 @@
     consts = [jnp.asarray(c) for c in tables(n)]
     anyspace = pl.BlockSpec(memory_space=pl.ANY)
     f32, bf16 = jnp.float32, jnp.bfloat16
-    return pl.pallas_call(
+    whole = (nt, ROUNDS, bins, 2, WIDE)
+    held = pl.pallas_call(
         functools.partial(kernel, n, nc, rows, nt),
         in_specs=[pl.BlockSpec(memory_space=pltpu.SMEM)] + [anyspace] * 6,
-        out_specs=anyspace,
-        out_shape=jax.ShapeDtypeStruct((ROUNDS, bins, 2, chans * SRC), f32),
+        out_specs=pl.BlockSpec(memory_space=pltpu.VMEM),
+        out_shape=pltpu.VMEM(whole, f32),
         scratch_shapes=[
             pltpu.VMEM((chans * rows, LANES), f32),
             *[pltpu.VMEM(c.shape, c.dtype) for c in consts],
@@ -398,20 +396,27 @@
             pltpu.VMEM((ROUNDS, bins, pack_width(n)), f32),
             pltpu.VMEM((ROUNDS, bins, 2 * n * LANES), f32),
             pltpu.VMEM((n * KB, 2 * WIDE), f32),
-            pltpu.VMEM((2, ROUNDS, KB, 2, WIDE), f32),
             pltpu.SemaphoreType.DMA((nt,)),
             pltpu.SemaphoreType.DMA((5,)),
             pltpu.SemaphoreType.DMA((nt, n - 1, nsub)),
             pltpu.SemaphoreType.DMA((nt, n - 1, nsub)),
             pltpu.SemaphoreType.DMA((ROUNDS,)),
             pltpu.SemaphoreType.DMA((ROUNDS,)),
-            pltpu.SemaphoreType.DMA((2,)),
         ],
         compiler_params=pltpu.CompilerParams(
-            collective_id=0, has_side_effects=True, vmem_limit_bytes=60 << 20
+            collective_id=0, has_side_effects=True, vmem_limit_bytes=59000 << 10
         ),
         name="correlate",
     )(offsets, flat, *consts)
+    return pl.pallas_call(
+        functools.partial(write_out, nt),
+        in_specs=[pl.BlockSpec(memory_space=pltpu.VMEM)],
+        out_specs=anyspace,
+        out_shape=jax.ShapeDtypeStruct((ROUNDS, bins, 2, chans * SRC), f32),
+        scratch_shapes=[pltpu.SemaphoreType.DMA((nt, ROUNDS))],
+        compiler_params=pltpu.CompilerParams(vmem_limit_bytes=8 << 20),
+        name="write",
+    )(held)
 
 
 def solution(mesh):

time: 55.2 us -> 49.4 us (0.89)
  local copies, waits for them, and re-layouts: 7.9 us -> 0 us
  Pallas kernels: 46.5 us -> 48.6 us
    unnamed x1 -> x0, local copies, waits for them, and re-layouts: 7.9 us -> none
    pallas_call x0 -> x1, Pallas kernels: none -> 2.83 us  [shards(): pl.pallas_call(functools.partial(write_out, nt), in_specs=[pl.BlockSpec(m...]
    pallas_call x1, Pallas kernels: 46.5 us -> 45.8 us  [shards(): pl.pallas_call(functools.partial(kernel, n, nc, rows, nt), in_specs=[pl.B...]
where the time goes in v1:
time: 49.4 us; the launch traced here: 49.3 us
  Pallas kernels  48.6 us (98%)
  between operations  0.66 us (1%)
    pallas_call x1, Pallas kernels, shards(): pl.pallas_call(functools.partial(kernel, n, nc, rows, nt), in_specs=[pl.B...  45.8 us
    pallas_call x1, Pallas kernels, shards(): pl.pallas_call(functools.partial(write_out, nt), in_specs=[pl.BlockSpec(m...  2.83 us

profile of v1, /device:TPU:0, one launch (start us, length us, event | category | flops | bytes accessed | tf_op | source)
XLA Modules:
  0.0 49.3 jit_solution(11772751472822526005)
XLA Ops:
  0.7 45.8 %correlate.1.x_ref = f32[5,2,160,2,512]{4,3,2,1,0:T(2,128)S(1)} custom-call(s32[1]{0:T(128)S(6)} %copy.8.off_ref, f32[19840,128]{1,0:T(8,128)} %bitcast.1, f32[14,8,512]{2,1,0:T(8,128)} %constant.10.clone.tw_hbm, bf16[192,512]{1,0:T(8,128)(2,1)} %constant.11.clone.both_hbm, bf16[640,640]{1,0:T(8,128)(2,1)} %constant.12.clone.band_hbm, ...), custom_call_target="tpu_custom_call" | custom-call | tf_op jit(solution)/shard_map/correlate/pallas_call | solution.py:382
  46.4 2.8 %write.1 = f32[2,160,2,2560]{3,2,1,0:T(2,128)} custom-call(f32[5,2,160,2,512]{4,3,2,1,0:T(2,128)S(1)} %correlate.1.x_ref), custom_call_target="tpu_custom_call" | custom-call | tf_op jit(solution)/shard_map/write/pallas_call | solution.py:411

commit v2 on v1

--- a/solution.py
+++ b/solution.py
@@ -28,6 +28,9 @@
 CT = 64
 WIDE = CT * SRC
 KB = 40
+STEP = 2 * SMOOTH
+FETCH = 16
+LATE = 2
 
 
 def split(x):
@@ -51,8 +54,9 @@
     turn = 2.0 * math.pi * (r[:, None] * a[None, :]) / LEN
     twiddle = np.stack([np.cos(turn), np.sin(turn)], 1).reshape(2 * len(r), L)
     twiddle = np.repeat(twiddle[:, None, :], 8, 1).astype(np.float32)
-    k = np.arange(FB)
-    band = (np.abs(k[:, None] - k[None, :]) <= SMOOTH).astype(jnp.bfloat16)
+    k = np.arange(STEP)[:, None]
+    col = np.arange(2 * STEP)[None, :]
+    band = np.stack([np.abs(k + shift - col) <= SMOOTH for shift in (0, SMOOTH, STEP)]).astype(jnp.bfloat16)
     lane = np.arange(LANES)[:, None]
     col = np.arange(2 * WIDE)[None, :]
     spread = lane == (col // WIDE) * CT + (col % WIDE) // SRC
@@ -112,7 +116,7 @@
     return bins
 
 
-def first_stage(rows, base, off, x_ref, twiddle_ref, hi_ref, lo_ref):
+def first_stage(rows, chunk, off, arrive, x_ref, twiddle_ref, hi_ref, lo_ref):
     lane = lax.broadcasted_iota(jnp.int32, (16, LANES), 1)
     extra = rows - PARTS
 
@@ -122,10 +126,13 @@
         lo_ref[pl.ds(row * CT + c0, 16), pl.ds(a0, LANES)] = lo
 
     def block(i, carry):
-        c0 = pl.multiple_of(i * 16, 16)
+        c0 = pl.multiple_of(i * FETCH, FETCH)
+        piece = chunk * (CT // FETCH) + i
+        if arrive is not None:
+            arrive(i)
 
         def load(j):
-            return x_ref[pl.ds(base + c0 * rows + j, 16, stride=rows), :]
+            return x_ref[pl.ds(piece * FETCH * rows + j, FETCH, stride=rows), :]
 
         for t in range(L // LANES):
             x = []
@@ -148,7 +155,7 @@
                 put(2 * r - 1, c0, a0, im * cos - re * sin)
         return carry
 
-    lax.fori_loop(0, CT // 16, block, 0)
+    lax.fori_loop(0, CT // FETCH, block, 0)
 
 
 def second_stage(both_ref, hi_ref, lo_ref, w_ref):
@@ -182,7 +189,12 @@
     high = amp.astype(jnp.bfloat16).astype(jnp.float32)
     low = lax.broadcasted_iota(jnp.int32, (FB, LANES), 1) < CT
     parts = jnp.where(low, high, amp - high).astype(jnp.bfloat16)
-    total = jnp.dot(band_ref[...], parts, preferred_element_type=jnp.float32)
+    total = []
+    for i in range(FB // STEP):
+        start = min(max(i * STEP - SMOOTH, 0), FB - 2 * STEP)
+        window = parts[start : start + 2 * STEP]
+        total.append(jnp.dot(band_ref[(i * STEP - start) // SMOOTH], window, preferred_element_type=jnp.float32))
+    total = jnp.concatenate(total, 0)
     total = total + pltpu.roll(total, CT, 1)
     k = lax.broadcasted_iota(jnp.int32, (FB, LANES), 0)
     count = jnp.minimum(k + SMOOTH, FB - 1) - jnp.maximum(k - SMOOTH, 0) + 1
@@ -190,27 +202,67 @@
     return spec * (count / (total + 1e-06 * count))
 
 
-def kernel(n, nc, rows, nt, off_ref, x_hbm, tw_hbm, both_hbm, band_hbm, spread_hbm, fan_hbm, o_ref,
-           x_ref, tw_ref, both_ref, band_ref, spread_ref, fan_ref, hi_ref, lo_ref, w_ref, white, recv,
-           src_send, src_recv, b_ref, a_ref,
-           x_sem, const_sem, send_sem, recv_sem, ssend_sem, srecv_sem):
+def combine(n, a, k0, a_ref, b_ref, spread_ref, put):
+    a_ref[...] = jnp.dot(twice(jnp.concatenate(a, 0)), spread_ref[...], preferred_element_type=jnp.float32)
+
+    def group(g, carry):
+        g8 = pl.multiple_of(g * 8, 8)
+        b = [[[b_ref[rnd, pl.ds(pl.multiple_of(k0 + g8, 8), 8), (2 * w + p) * LANES : (2 * w + p + 1) * LANES]
+               for p in range(2)] for w in range(n)] for rnd in range(ROUNDS)]
+        for tile in range(WIDE // LANES):
+            lanes = slice(tile * LANES, (tile + 1) * LANES)
+            far = slice(WIDE + tile * LANES, WIDE + (tile + 1) * LANES)
+            ar = [a_ref[pl.ds(w * KB + g8, 8), lanes] for w in range(n)]
+            ai = [a_ref[pl.ds(w * KB + g8, 8), far] for w in range(n)]
+            for rnd in range(ROUNDS):
+                real = imag = None
+                for w in range(n):
+                    br, bi = b[rnd][w]
+                    p = ar[w] * br + ai[w] * bi
+                    q = ai[w] * br - ar[w] * bi
+                    real = p if real is None else real + p
+                    imag = q if imag is None else imag + q
+                put(rnd, g8, 0, lanes, real)
+                put(rnd, g8, 1, lanes, imag)
+        return carry
+
+    lax.fori_loop(0, KB // 8, group, 0)
+
+
+def kernel(n, nc, rows, nt, off_hbm, x_hbm, tw_hbm, both_hbm, band_hbm, spread_hbm, fan_hbm,
+           o_ref, late_ref, b_ref, spread_ref,
+           off_ref, x_ref, tw_ref, both_ref, band_ref, fan_ref, hi_ref, lo_ref, w_ref, white, recv,
+           src_send, src_recv, a_ref,
+           off_sem, x_sem, const_sem, send_sem, recv_sem, ssend_sem, srecv_sem):
     me = lax.axis_index("tm")
     blk = lax.axis_index("chan")
     bins = FB // n
     nsub = bins // KB
-    off = off_ref[0]
-
-    def fetch(t):
-        part = pl.ds(t * CT * rows, CT * rows)
-        return pltpu.make_async_copy(x_hbm.at[part, :], x_ref.at[part, :], x_sem.at[t])
+
+    first = CT // FETCH
+
+    def fetch(start, size, sem):
+        part = pl.ds(pl.multiple_of(start * rows, 8), size * rows)
+        return pltpu.make_async_copy(x_hbm.at[part, :], x_ref.at[part, :], x_sem.at[sem])
+
+    def piece(i):
+        return fetch(i * FETCH, FETCH, i)
+
+    def chunk(t):
+        return fetch(t * CT, CT, first - 1 + t)
 
     pairs = ((tw_hbm, tw_ref), (both_hbm, both_ref), (band_hbm, band_ref), (spread_hbm, spread_ref), (fan_hbm, fan_ref))
     consts = [pltpu.make_async_copy(src, dst, const_sem.at[i]) for i, (src, dst) in enumerate(pairs)]
-    fetch(0).start()
-    for c in consts[:3]:
+    shift = pltpu.make_async_copy(off_hbm, off_ref, off_sem.at[0])
+    piece(0).start()
+    consts[0].start()
+    shift.start()
+    for i in range(1, first):
+        piece(i).start()
+    for c in consts[1:3]:
         c.start()
     for t in range(1, nt):
-        fetch(t).start()
+        chunk(t).start()
     for c in consts[3:]:
         c.start()
 
@@ -221,55 +273,62 @@
     for s in chan_steps:
         pl.semaphore_signal(barrier, inc=1, device_id={"chan": lax.rem(blk + s, nc)}, device_id_type=MESH)
 
-    def exchange(t, j, sh):
+    def exchange(t, part, sh):
         peer = lax.rem(me + sh, n)
+        sem, k, size = part
         return pltpu.make_async_remote_copy(
-            src_ref=white.at[t, pl.ds(pl.multiple_of(peer * bins + j * KB, 8), KB), :],
-            dst_ref=recv.at[sh - 1, t, pl.ds(pl.multiple_of(j * KB, 8), KB), :],
-            send_sem=send_sem.at[t, sh - 1, j],
-            recv_sem=recv_sem.at[t, sh - 1, j],
+            src_ref=white.at[t, pl.ds(pl.multiple_of(peer * bins + k, 8), size), :],
+            dst_ref=recv.at[sh - 1, t, pl.ds(pl.multiple_of(k, 8), size), :],
+            send_sem=send_sem.at[t, sh - 1, sem],
+            recv_sem=recv_sem.at[t, sh - 1, sem],
             device_id={"tm": peer},
             device_id_type=MESH,
         )
 
     order = list(range(2, n)) + [1]
-
-    def transform(t, carry):
-        fetch(t).wait()
-
-        @pl.when(t == 0)
+    late = late_ref.shape[1]
+    early = bins - late
+    entire = (0, 0, bins)
+    parts = [(j, j * KB, KB) for j in range(early // KB)] + [(early // KB, early, late)]
+
+    def transform(t, arrive):
+        first_stage(rows, t, off_ref[0], arrive, x_ref, tw_ref, hi_ref, lo_ref)
+        if arrive is not None:
+            consts[1].wait()
+        second_stage(both_ref, hi_ref, lo_ref, w_ref)
+        if arrive is not None:
+            consts[2].wait()
+        white[t] = normalised(band_ref, w_ref)
+
+    consts[0].wait()
+    shift.wait()
+    transform(0, lambda i: piece(i).wait())
+    pl.semaphore_wait(barrier, n - 1 + len(chan_steps))
+    for sh in order:
+        exchange(0, entire, sh).start()
+
+    def later(t, carry):
+        chunk(t).wait()
+        transform(t, None)
+
+        @pl.when(t < nt - 1)
         def _():
-            consts[0].wait()
-
-        first_stage(rows, t * CT * rows, off, x_ref, tw_ref, hi_ref, lo_ref)
-
-        @pl.when(t == 0)
+            for sh in order:
+                exchange(t, entire, sh).start()
+
+        @pl.when(t == nt - 1)
         def _():
-            consts[1].wait()
-
-        second_stage(both_ref, hi_ref, lo_ref, w_ref)
-
-        @pl.when(t == 0)
-        def _():
-            consts[2].wait()
-
-        white[t] = normalised(band_ref, w_ref)
-
-        @pl.when(t == 0)
-        def _():
-            pl.semaphore_wait(barrier, n - 1 + len(chan_steps))
-
-        for j in range(nsub):
-            for sh in order:
-                exchange(t, j, sh).start()
+            for part in parts:
+                for sh in order:
+                    exchange(t, part, sh).start()
+
         return carry
 
-    lax.fori_loop(0, nt, transform, 0)
+    lax.fori_loop(1, nt, later, 0)
 
     mine = pl.multiple_of(me * bins, 8)
-    for j in range(nsub):
-        for sh in order:
-            exchange(0, j, sh).wait_recv()
+    for sh in order:
+        exchange(0, entire, sh).wait_recv()
     lane = lax.broadcasted_iota(jnp.int32, (bins, LANES), 1)
     for tile in range(src_send.shape[1] // LANES):
         packed = jnp.zeros((bins, LANES), jnp.float32)
@@ -306,62 +365,69 @@
         t = lax.div(u, nsub)
         j = lax.rem(u, nsub)
 
-        @pl.when(t > 0)
+        @pl.when((t > 0) & (t < nt - 1) & (j == 0))
         def _():
             for sh in order:
-                exchange(t, j, sh).wait_recv()
+                exchange(t, entire, sh).wait_recv()
+
+        @pl.when(t == nt - 1)
+        def _():
+            for sh in order:
+                exchange(t, (j, j * KB, KB), sh).wait_recv()
 
         k0 = pl.multiple_of(j * KB, 8)
         a = [white[t, pl.ds(pl.multiple_of(mine + k0, 8), KB), :]]
         a += [recv[sh - 1, t, pl.ds(k0, KB), :] for sh in range(1, n)]
-        a_ref[...] = jnp.dot(twice(jnp.concatenate(a, 0)), spread_ref[...], preferred_element_type=jnp.float32)
-
-        def group(g, carry):
-            g8 = pl.multiple_of(g * 8, 8)
-            b = [[[b_ref[rnd, pl.ds(pl.multiple_of(k0 + g8, 8), 8), (2 * w + p) * LANES : (2 * w + p + 1) * LANES]
-                   for p in range(2)] for w in range(n)] for rnd in range(ROUNDS)]
-            for tile in range(WIDE // LANES):
-                lanes = slice(tile * LANES, (tile + 1) * LANES)
-                far = slice(WIDE + tile * LANES, WIDE + (tile + 1) * LANES)
-                ar = [a_ref[pl.ds(w * KB + g8, 8), lanes] for w in range(n)]
-                ai = [a_ref[pl.ds(w * KB + g8, 8), far] for w in range(n)]
-                for rnd in range(ROUNDS):
-                    real = imag = None
-                    for w in range(n):
-                        br, bi = b[rnd][w]
-                        p = ar[w] * br + ai[w] * bi
-                        q = ai[w] * br - ar[w] * bi
-                        real = p if real is None else real + p
-                        imag = q if imag is None else imag + q
-                    o_ref[t, rnd, pl.ds(pl.multiple_of(k0 + g8, 8), 8), 0, lanes] = real
-                    o_ref[t, rnd, pl.ds(pl.multiple_of(k0 + g8, 8), 8), 1, lanes] = imag
-            return carry
-
-        lax.fori_loop(0, KB // 8, group, 0)
+
+        def put(rnd, k, part, lanes, value):
+            o_ref[t, rnd, pl.ds(pl.multiple_of(k0 + k, 8), 8), part, lanes] = value
+
+        combine(n, a, k0, a_ref, b_ref, spread_ref, put)
         return carry
 
-    lax.fori_loop(0, nt * nsub, pairing, 0)
+    lax.fori_loop(0, nt * nsub - late // KB, pairing, 0)
+    for sh in order:
+        exchange(nt - 1, parts[-1], sh).wait_recv()
+    late_ref[0] = white[nt - 1, pl.ds(pl.multiple_of(mine + early, 8), late), :]
+    for sh in range(1, n):
+        late_ref[sh] = recv[sh - 1, nt - 1, early:, :]
 
     for r in range(1, ROUNDS + 1):
         source(r).wait_send()
 
     def drain(t, carry):
-        for j in range(nsub):
-            for sh in order:
-                exchange(t, j, sh).wait_send()
+        for sh in order:
+            exchange(t, entire, sh).wait_send()
         return carry
 
-    lax.fori_loop(0, nt, drain, 0)
-
-
-def write_out(nt, x_ref, o_hbm, sem):
-    copies = [
-        pltpu.make_async_copy(x_ref.at[t, rnd], o_hbm.at[rnd, :, :, pl.ds(t * WIDE, WIDE)], sem.at[t, rnd])
-        for t in range(nt)
-        for rnd in range(ROUNDS)
-    ]
+    lax.fori_loop(0, nt - 1, drain, 0)
+    for part in parts:
+        for sh in order:
+            exchange(nt - 1, part, sh).wait_send()
+
+
+def write_out(n, nt, x_ref, late_ref, b_ref, spread_ref, o_hbm, a_ref, stage, sem, late_sem):
+    bins, late = b_ref.shape[1], late_ref.shape[1]
+    early = bins - late
+    copies = []
+    for t in range(nt):
+        size = bins if t < nt - 1 else early
+        for rnd in range(ROUNDS if size else 0):
+            part = pl.ds(0, size)
+            to = o_hbm.at[rnd, part, :, pl.ds(t * WIDE, WIDE)]
+            copies.append(pltpu.make_async_copy(x_ref.at[t, rnd, part], to, sem.at[t, rnd]))
     for c in copies:
         c.start()
+    for j in range(late // KB):
+        a = [late_ref[w, j * KB : (j + 1) * KB, :] for w in range(n)]
+
+        def put(rnd, k, part, lanes, value):
+            stage[j, rnd, pl.ds(k, 8), part, lanes] = value
+
+        combine(n, a, early + j * KB, a_ref, b_ref, spread_ref, put)
+        to = o_hbm.at[:, pl.ds(early + j * KB, KB), :, pl.ds((nt - 1) * WIDE, WIDE)]
+        copies.append(pltpu.make_async_copy(stage.at[j], to, late_sem.at[j]))
+        copies[-1].start()
     for c in copies:
         c.wait()
 
@@ -373,20 +439,28 @@
     nt = chans // CT
     bins = FB // n
     nsub = bins // KB
-    assert records.shape[1] == 1 and chans % CT == 0 and bins % KB == 0
+    assert records.shape[1] == 1 and chans % CT == 0 and bins % KB == 0 and nt > 1
     flat = records.reshape(chans * rows, LANES)
     consts = [jnp.asarray(c) for c in tables(n)]
     anyspace = pl.BlockSpec(memory_space=pl.ANY)
     f32, bf16 = jnp.float32, jnp.bfloat16
     whole = (nt, ROUNDS, bins, 2, WIDE)
+    late = min(LATE, nsub)
+    vmem = pl.BlockSpec(memory_space=pltpu.VMEM)
     held = pl.pallas_call(
         functools.partial(kernel, n, nc, rows, nt),
-        in_specs=[pl.BlockSpec(memory_space=pltpu.SMEM)] + [anyspace] * 6,
-        out_specs=pl.BlockSpec(memory_space=pltpu.VMEM),
-        out_shape=pltpu.VMEM(whole, f32),
+        in_specs=[pl.BlockSpec(memory_space=pltpu.HBM)] + [anyspace] * 6,
+        out_specs=[vmem] * 4,
+        out_shape=[
+            pltpu.VMEM(whole, f32),
+            pltpu.VMEM((n, late * KB, LANES), f32),
+            pltpu.VMEM((ROUNDS, bins, 2 * n * LANES), f32),
+            pltpu.VMEM(consts[3].shape, bf16),
+        ],
         scratch_shapes=[
+            pltpu.SMEM((1,), jnp.int32),
             pltpu.VMEM((chans * rows, LANES), f32),
-            *[pltpu.VMEM(c.shape, c.dtype) for c in consts],
+            *[pltpu.VMEM(c.shape, c.dtype) for i, c in enumerate(consts) if i != 3],
             pltpu.VMEM((M * CT, L), bf16),
             pltpu.VMEM((M * CT, L), bf16),
             pltpu.VMEM((ROWS + 8, LANES), f32),
@@ -394,9 +468,9 @@
             pltpu.VMEM((n - 1, nt, bins, LANES), f32),
             pltpu.VMEM((bins, pack_width(n)), f32),
             pltpu.VMEM((ROUNDS, bins, pack_width(n)), f32),
-            pltpu.VMEM((ROUNDS, bins, 2 * n * LANES), f32),
             pltpu.VMEM((n * KB, 2 * WIDE), f32),
-            pltpu.SemaphoreType.DMA((nt,)),
+            pltpu.SemaphoreType.DMA((1,)),
+            pltpu.SemaphoreType.DMA((nt + CT // FETCH,)),
             pltpu.SemaphoreType.DMA((5,)),
             pltpu.SemaphoreType.DMA((nt, n - 1, nsub)),
             pltpu.SemaphoreType.DMA((nt, n - 1, nsub)),
@@ -404,19 +478,24 @@
             pltpu.SemaphoreType.DMA((ROUNDS,)),
         ],
         compiler_params=pltpu.CompilerParams(
-            collective_id=0, has_side_effects=True, vmem_limit_bytes=59000 << 10
+            collective_id=0, has_side_effects=True, vmem_limit_bytes=57050 << 10
         ),
         name="correlate",
     )(offsets, flat, *consts)
     return pl.pallas_call(
-        functools.partial(write_out, nt),
-        in_specs=[pl.BlockSpec(memory_space=pltpu.VMEM)],
+        functools.partial(write_out, n, nt),
+        in_specs=[vmem] * 4,
         out_specs=anyspace,
         out_shape=jax.ShapeDtypeStruct((ROUNDS, bins, 2, chans * SRC), f32),
-        scratch_shapes=[pltpu.SemaphoreType.DMA((nt, ROUNDS))],
-        compiler_params=pltpu.CompilerParams(vmem_limit_bytes=8 << 20),
+        scratch_shapes=[
+            pltpu.VMEM((n * KB, 2 * WIDE), f32),
+            pltpu.VMEM((late, ROUNDS, KB, 2, WIDE), f32),
+            pltpu.SemaphoreType.DMA((nt, ROUNDS)),
+            pltpu.SemaphoreType.DMA((late,)),
+        ],
+        compiler_params=pltpu.CompilerParams(vmem_limit_bytes=10 << 20),
         name="write",
-    )(held)
+    )(*held)
 
 
 def solution(mesh):

time: 49.4 us -> 48.1 us (0.974)
  Pallas kernels: 48.6 us -> 47.3 us
    pallas_call x1, Pallas kernels: 45.8 us -> 44.5 us  [shards(): pl.pallas_call(functools.partial(kernel, n, nc, rows, nt), in_specs=[pl.B...]
where the time goes in v2:
time: 48.1 us; the launch traced here: 48 us
  Pallas kernels  47.3 us (98%)
  between operations  0.66 us (1%)
    pallas_call x1, Pallas kernels, shards(): pl.pallas_call(functools.partial(kernel, n, nc, rows, nt), in_specs=[pl.B...  44.5 us
    pallas_call x1, Pallas kernels, shards(): pl.pallas_call(functools.partial(write_out, n, nt), in_specs=[vmem] * 4,...  2.85 us

profile of v2, /device:TPU:0, one launch (start us, length us, event | category | flops | bytes accessed | tf_op | source)
XLA Modules:
  0.0 48.0 jit_solution(39539867685450610)
XLA Ops:
  0.7 44.5 %correlate.1 = (f32[5,2,160,2,512]{4,3,2,1,0:T(2,128)S(1)}, f32[4,80,128]{2,1,0:T(8,128)S(1)}, f32[2,160,1024]{2,1,0:T(8,128)S(1)}, bf16[256,1024]{1,0:T(8,128)(2,1)S(1)}) custom-call(s32[1]{0:T(128)S(6)} %copy.8.off_hbm, f32[19840,128]{1,0:T(8,128)} %bitcast.1, f32[14,8,512]{2,1,0:T(8,128)} %constant.10.clone.tw_hbm, ...), custom_call_target="tpu_custom_call" | custom-call | tf_op jit(solution)/shard_map/correlate/pallas_call | solution.py:450
  45.1 2.9 %write.1 = f32[2,160,2,2560]{3,2,1,0:T(2,128)} custom-call(f32[5,2,160,2,512]{4,3,2,1,0:T(2,128)S(1)} %get-tuple-element.9.x_ref, f32[4,80,128]{2,1,0:T(8,128)S(1)} %get-tuple-element.10.late_ref, f32[2,160,1024]{2,1,0:T(8,128)S(1)} %get-tuple-element.11.b_ref, bf16[256,1024]{1,0:T(8,128)(2,1)S(1)} %get-tuple-element.12.spread_ref), custom_call_target="tpu_custom_call" | custom-call | tf_op jit(solution)/shard_map/write/pallas_call | solution.py:485
